TPU v7x, 256 devices: a whole 4x4x8 slice. The times are simulated.
256 devices in a mesh: tm: 16 (over x_hi, z), tensor: 16 (over x_lo, y, core).
Axes of the slice: x: 4 (x_hi: 2, x_lo: 2; x = x_hi * 2 + x_lo), y: 4, z: 8, core: 2. Of those that a mesh axis runs over, the one named last changes fastest.
Arguments:
- features: bfloat16 [2, 2048, 1536], P(None, 'tm'), may hold values from -6 to 6
- lengths: int32 [2], replicated, may hold values from 512 to 2048, as said below
- norm_gains: float32 [2, 1536], replicated, may hold values from 0.1 to 1.9
- qkv_weight: bfloat16 [3, 1536, 1536], P(None, 'tensor'), may hold values from -0.21650635 to 0.21650635
- pos_weight: bfloat16 [1536, 1536], P('tensor'), may hold values from -0.15625 to 0.15625
- pos_biases: float32 [2, 1536], P(None, 'tensor'), may hold values from -3 to 3
- out_weight: bfloat16 [1536, 1536], P('tensor'), may hold values from -0.15625 to 0.15625
- conv_in_weight: bfloat16 [2, 1536, 1536], P(None, 'tensor'), may hold values from -0.15625 to 0.15625
- depth_kernel: float32 [31, 1536], P(None, 'tensor'), may hold values from -1 to 1
- conv_scale: float32 [1536], P('tensor'), may hold values from 0.1 to 1.9
- conv_shift: float32 [1536], P('tensor'), may hold values from -3 to 3
- conv_out_weight: bfloat16 [1536, 1536], P('tensor'), may hold values from -0.15625 to 0.15625
Outputs:
- encoded: bfloat16 [2, 2048, 1536], P(None, ('tm', 'tensor'))
Inputs may be any that keep to these rules, and one draw needn't show every extreme that they name: `lengths`: the first window is whole.
All inputs are finite; a program needn't handle non-finite values.
Results may differ from a plain program's by a relative error of at most 0.017.
Values may be sent and summed in bfloat16 or wider, within the bound.
A program may use at most 64 MiB of HBM per device.

v0:
```python
import math
import jax
import jax.numpy as jnp
from jax import lax
from jax.sharding import PartitionSpec as P

HD = 96
epsilon = 1e-05


def padded_2(cells, sides, width):
    for axis, dim in sides:
        count = lax.axis_size(axis)
        ends = count - 1
        head = lax.slice_in_dim(cells, 0, width, axis=dim)
        tail = lax.slice_in_dim(cells, cells.shape[dim] - width, cells.shape[dim], axis=dim)
        cells = jnp.concatenate(
            [
                lax.ppermute(tail, axis, [(i, (i + 1) % count) for i in range(ends)]),
                cells,
                lax.ppermute(head, axis, [((i + 1) % count, i) for i in range(ends)]),
            ],
            axis=dim,
        )
    return cells


def layer_norm(values, gain):
    values = values.astype(jnp.float32)
    row_mean = jnp.mean(values, axis=-1, keepdims=True)
    centred = values - row_mean
    variance = jnp.mean(centred * centred, axis=-1, keepdims=True)
    return centred * lax.rsqrt(variance + epsilon) * gain


def positions(offsets, model_width, pos_weight):
    half_width = model_width // 2
    frequency = jnp.exp(
        jnp.arange(half_width, dtype=jnp.float32) * (-2.0 * math.log(10000.0) / model_width)
    )
    angles = offsets.astype(jnp.float32)[:, None] * frequency[None, :]
    pos_table = jnp.concatenate(
        [jnp.sin(angles).astype(jnp.bfloat16), jnp.cos(angles).astype(jnp.bfloat16)], axis=1
    )
    return jnp.einsum(
        "md,cd->mc", pos_table, pos_weight, preferred_element_type=jnp.float32
    ).astype(jnp.bfloat16)


def diagonal_take(pos_table, row_count, col_count):
    table_width = pos_table.shape[-1]
    leading = pos_table.shape[:-2]
    flattened = pos_table.reshape(leading + (row_count * table_width,))
    flattened = lax.slice_in_dim(
        flattened,
        row_count - 1,
        row_count - 1 + row_count * (table_width - 1),
        axis=flattened.ndim - 1,
    )
    return flattened.reshape(leading + (row_count, table_width - 1))[..., :col_count]


def shards(
    features,
    lengths,
    norm_gains,
    qkv_weight,
    pos_weight,
    pos_biases,
    out_weight,
    conv_in_weight,
    depth_kernel,
    conv_scale,
    conv_shift,
    conv_out_weight,
):
    windows, local_rows, model_width = features.shape
    channels = qkv_weight.shape[1]
    heads_here = channels // HD
    score_scale = 1.0 / math.sqrt(HD)
    first_frame = lax.axis_index("tm") * local_rows
    frame_ids = first_frame + jnp.arange(local_rows, dtype=jnp.int32)
    normed = layer_norm(features, norm_gains[0]).astype(jnp.bfloat16)
    projections = jnp.einsum(
        "btd,gcd->btgc", normed, qkv_weight, preferred_element_type=jnp.float32
    )
    query_all = projections[:, :, 0]
    content_q = (
        (query_all + pos_biases[0])
        .astype(jnp.bfloat16)
        .reshape(windows, local_rows, heads_here, HD)
    )
    position_q = (
        (query_all + pos_biases[1])
        .astype(jnp.bfloat16)
        .reshape(windows, local_rows, heads_here, HD)
    )
    key_rows = projections[:, :, 1].astype(jnp.bfloat16)
    value_rows = projections[:, :, 2].astype(jnp.bfloat16)
    global_frames = local_rows * lax.axis_size("tm")
    table_rows = global_frames + local_rows - 1
    all_offsets = first_frame + local_rows - 1 - jnp.arange(table_rows, dtype=jnp.int32)
    relative_all = positions(all_offsets, model_width, pos_weight).reshape(
        table_rows, heads_here, HD
    )
    running_max = jnp.full((windows, heads_here, local_rows), -1e30, jnp.float32)
    key_piece = lax.all_gather(key_rows, "tm", axis=1, tiled=True)
    value_piece = lax.all_gather(value_rows, "tm", axis=1, tiled=True)
    key_count = key_piece.shape[1]
    key_heads = key_piece.reshape(windows, key_count, heads_here, HD)
    value_heads = value_piece.reshape(windows, key_count, heads_here, HD)
    content_scores = jnp.einsum(
        "bqhe,bkhe->bhqk", content_q, key_heads, preferred_element_type=jnp.float32
    )
    full_pos = jnp.einsum(
        "bqhe,mhe->bhqm", position_q, relative_all, preferred_element_type=jnp.float32
    )
    scores = (content_scores + diagonal_take(full_pos, local_rows, key_count)) * score_scale
    key_ids = jnp.arange(key_count, dtype=jnp.int32)
    key_mask = (key_ids[None, :] < lengths[:, None])[:, None, None, :]
    scores = jnp.where(key_mask, scores, -1e30)
    new_max = jnp.maximum(running_max, jnp.max(scores, axis=-1))
    attention_weights = jnp.where(key_mask, jnp.exp(scores - new_max[..., None]), 0.0)
    running_sum = jnp.sum(attention_weights, axis=-1)
    weighted = jnp.einsum(
        "bhqk,bkhe->bhqe",
        attention_weights.astype(jnp.bfloat16),
        value_heads,
        preferred_element_type=jnp.float32,
    )
    head_outputs = (weighted / running_sum[..., None]).astype(jnp.bfloat16)
    head_outputs = head_outputs.transpose(0, 2, 1, 3).reshape(windows, local_rows, channels)
    attention_term = jnp.einsum(
        "btc,cd->btd", head_outputs, out_weight, preferred_element_type=jnp.float32
    )
    row_count = local_rows // lax.axis_size("tensor")
    row_start = lax.axis_index("tensor") * row_count
    attention_full = lax.psum(attention_term.astype(jnp.bfloat16), "tensor").astype(jnp.float32)
    hidden = (features.astype(jnp.float32) + attention_full).astype(jnp.bfloat16)
    hidden_rows = lax.dynamic_slice_in_dim(hidden, row_start, row_count, 1)
    normed_two = layer_norm(hidden, norm_gains[1]).astype(jnp.bfloat16)
    widened = jnp.einsum(
        "btd,gcd->btgc", normed_two, conv_in_weight, preferred_element_type=jnp.float32
    )
    gated_units = widened[:, :, 0] * jax.nn.sigmoid(widened[:, :, 1])
    frame_valid = frame_ids[None, :] < lengths[:, None]
    gated_units = jnp.where(frame_valid[:, :, None], gated_units, 0.0).astype(jnp.bfloat16)
    rim = depth_kernel.shape[0] // 2
    padded = padded_2(gated_units, (("tm", 1),), rim)
    depth_sum = jnp.zeros(gated_units.shape, jnp.float32)
    for tap_index in range(depth_kernel.shape[0]):
        depth_sum = (
            depth_sum
            + padded[:, tap_index : tap_index + local_rows].astype(jnp.float32)
            * depth_kernel[tap_index]
        )
    affine = depth_sum * conv_scale + conv_shift
    activated = (affine * jax.nn.sigmoid(affine)).astype(jnp.bfloat16)
    conv_term = jnp.einsum(
        "btc,cd->btd", activated, conv_out_weight, preferred_element_type=jnp.float32
    )
    conv_rows = lax.psum_scatter(
        conv_term.astype(jnp.bfloat16), "tensor", scatter_dimension=1, tiled=True
    ).astype(jnp.float32)
    return (hidden_rows.astype(jnp.float32) + conv_rows).astype(jnp.bfloat16)


def solution(mesh):
    return jax.shard_map(
        shards,
        mesh=mesh,
        in_specs=(
            P(None, "tm", None),
            P(),
            P(),
            P(None, "tensor", None),
            P("tensor", None),
            P(None, "tensor"),
            P("tensor", None),
            P(None, "tensor", None),
            P(None, "tensor"),
            P("tensor"),
            P("tensor"),
            P("tensor", None),
        ),
        out_specs=P(None, ("tm", "tensor"), None),
        check_vma=False,
    )
```

profile of v0, /device:TPU:4, one launch (start us, length us, event | category | flops | bytes accessed | tf_op | source)
XLA Modules:
  0.0 364.2 jit_solution(17981048727000011265)
XLA Ops:
  6.5 0.8 slice_reduce_fusion
  7.4 1.3 convert_reduce_fusion
  8.7 1.5 fusion.21
  10.2 0.8 slice_bitcast_fusion.32
  11.0 26.0 %fusion = (bf16[2175,768]{1,0:T(8,128)(2,1)}, bf16[2175,768]{1,0:T(8,128)(2,1)}) fusion(f32[768]{0:T(1024)S(1)} %multiply_exponential_fusion, f32[2175]{0:T(1024)S(1)} %subtract_convert_fusion), kind=kLoop, calls=%fused_computation.2 | loop fusion | flops 5011200 | bytes 6693372 | tf_op jit(solution)/shard_map/convert_element_type | solution.py:43
  38.3 6.8 %convolution_bitcast_fusion = f32[2,1,128,2175]{2,3,0,1:T(8,128)} fusion(bf16[96,1536]{1,0:T(8,128)(2,1)S(1)} %copy-done.7, bf16[2175,768]{1,0:T(8,128)(2,1)} %get-tuple-element.45, bf16[2175,768]{1,0:T(8,128)(2,1)} %get-tuple-element.44, f32[2,128,3,96]{1,3,2,0:T(8,128)S(1)} %get-tuple-element.49, f32[96]{0:T(128)S(1)} %get-tuple-element.47), kind=kOutput, calls=%fused_computation.8 | convolution fusion | flops 761960320 | bytes 9302528 | tf_op jit(solution)/shard_map/bqhe,mhe->bhqm/dot_general | solution.py:115
  45.1 2.0 copy.14
  47.1 4.4 %reshape.176 = f32[2,1,278400]{2,0,1:T(2,128)} reshape(f32[2,1,128,2175]{3,2,0,1:T(8,128)S(1)} %copy.14) | data formatting | bytes 4454400 | tf_op jit(solution)/shard_map/reshape | solution.py:53
  51.5 3.9 %slice.330 = f32[2,1,278272]{2,0,1:T(2,128)S(1)} slice(f32[2,1,278400]{2,0,1:T(2,128)} %reshape.176), slice={[0:2], [0:1], [127:278399]} | slice | bytes 4452352 | tf_op jit(solution)/shard_map/slice | solution.py:54
  55.5 4.5 %reshape.177 = f32[2,1,128,2174]{3,2,0,1:T(8,128)} reshape(f32[2,1,278272]{2,0,1:T(2,128)S(1)} %slice.330) | data formatting | bytes 4452352 | tf_op jit(solution)/shard_map/reshape | solution.py:60
  59.9 46.0 %all-gather = bf16[2,2048,1,96]{1,3,2,0:T(8,128)(2,1)S(1)} all-gather(bf16[2,128,1,96]{1,3,2,0:T(8,128)(2,1)S(1)} %get-tuple-element.10), channel_id=2, replica_groups=mesh['tm'=16,'tensor'=16] {'tm'}, dimensions={1}, use_global_device_ids=true | all-gather | bytes 835584 | tf_op jit(solution)/shard_map/all_gather | solution.py:107
  106.0 2.4 fusion.172
  108.4 42.4 %all-gather.1 = bf16[2,2048,1,96]{1,3,2,0:T(8,128)(2,1)} all-gather(bf16[2,128,1,96]{1,3,2,0:T(8,128)(2,1)S(1)} %get-tuple-element.9), channel_id=3, replica_groups=mesh['tm'=16,'tensor'=16] {'tm'}, dimensions={1}, use_global_device_ids=true | all-gather | bytes 835584 | tf_op jit(solution)/shard_map/all_gather | solution.py:108
  151.4 2.9 convolution_convert_fusion.1
  154.5 122.0 %all-reduce.2.cloned.1.call-done = bf16[2,128,1536]{2,1,0:T(8,128)(2,1)} async-done(((bf16[2,128,1536]{2,1,0:T(8,128)(2,1)}), bf16[2,128,1536]{2,1,0:T(8,128)(2,1)}) %all-reduce.2.cloned.1.call-update) | async-done | bytes 786448 | tf_op jit(solution)/shard_map/psum | solution.py:138
  276.4 1.7 convert_reduce_fusion.1
  279.2 3.5 collective-permute-start
  282.7 6.0 %collective-permute-start.1 = (bf16[2,15,96]{1,2,0:T(8,128)(2,1)S(1)}, bf16[2,15,96]{1,2,0:T(8,128)(2,1)S(1)}, u32[]{:S(2)}, u32[]{:S(2)}) collective-permute-start(bf16[2,15,96]{1,2,0:T(8,128)(2,1)S(1)} %get-tuple-element.12), channel_id=1, source_target_pairs={{16,0},{32,16},{48,32},{64,48},{80,64},{96,80},{112,96},{128,112},... | collective-permute-start | bytes 17288 | tf_op jit(solution)/shard_map/ppermute | solution.py:21
  288.8 1.6 collective-permute-done.1
  290.4 1.7 convolution_convert_fusion
  292.1 0.8 copy.17
  292.9 1.0 copy.19
  293.9 62.0 %reduce-scatter.4.cloned.1.call-done = bf16[8,3072]{1,0:T(8,128)(2,1)} async-done(((bf16[128,3072]{1,0:T(8,128)(2,1)}), bf16[8,3072]{1,0:T(8,128)(2,1)}) %reduce-scatter.4.cloned.1.call-update) | async-done | bytes 49168
  355.9 0.8 reshape.190
  (47 shorter events, 3.9 us)
Async XLA Ops:
  6.5 30.5 %copy-start = (bf16[3,96,1536]{2,1,0:T(8,128)(2,1)S(1)}, bf16[3,96,1536]{2,1,0:T(8,128)(2,1)}, u32[]{:S(2)}) copy-start(bf16[3,96,1536]{2,1,0:T(8,128)(2,1)} %param.15) | copy-start | bytes 2654212
  6.5 269.9 %all-reduce.2.cloned.1.call-start = ((), (), s32[]{:S(2)}) async-start(), calls=%async_computation.1 | async-start | bytes 1572864 | tf_op jit(solution)/shard_map/psum | solution.py:138
  11.0 26.0 %copy-start.1 = (bf16[2,128,1536]{2,1,0:T(8,128)(2,1)S(1)}, bf16[2,128,1536]{2,1,0:T(8,128)(2,1)}, u32[]{:S(2)}) copy-start(bf16[2,128,1536]{2,1,0:T(8,128)(2,1)} %param.12) | copy-start | bytes 2359300
  37.0 1.3 copy-start.7
  37.6 0.7 copy-start.3
  55.4 50.5 %copy-start.5 = (s32[2]{0:T(128)S(1)}, s32[2]{0:T(128)}, u32[]{:S(2)}) copy-start(s32[2]{0:T(128)} %param.13) | copy-start | bytes 28
  108.4 43.0 %copy-start.2 = (bf16[96,1536]{1,0:T(8,128)(2,1)S(1)}, bf16[96,1536]{1,0:T(8,128)(2,1)}, u32[]{:S(2)}) copy-start(bf16[96,1536]{1,0:T(8,128)(2,1)} %param.18) | copy-start | bytes 884740
  151.4 3.1 copy-start.4
  154.3 124.2 %copy-start.6 = (bf16[2,96,1536]{2,1,0:T(8,128)(2,1)S(1)}, bf16[2,96,1536]{2,1,0:T(8,128)(2,1)}, u32[]{:S(2)}) copy-start(bf16[2,96,1536]{2,1,0:T(8,128)(2,1)} %param.19) | copy-start | bytes 1769476
  154.3 201.6 %reduce-scatter.4.cloned.1.call-start = ((), (), s32[]{:S(2)}) async-start(), calls=%async_computation.2 | async-start | bytes 835584
  278.1 12.3 %copy-start.8 = (bf16[96,1536]{1,0:T(8,128)(2,1)S(1)}, bf16[96,1536]{1,0:T(8,128)(2,1)}, u32[]{:S(2)}) copy-start(bf16[96,1536]{1,0:T(8,128)(2,1)} %param.23) | copy-start | bytes 884740
  278.1 12.3 %copy-start.9 = (f32[96]{0:T(128)S(1)}, f32[96]{0:T(128)}, u32[]{:S(2)}) copy-start(f32[96]{0:T(128)} %param.22) | copy-start | bytes 1156
  278.1 12.3 %copy-start.10 = (f32[96]{0:T(128)S(1)}, f32[96]{0:T(128)}, u32[]{:S(2)}) copy-start(f32[96]{0:T(128)} %param.21) | copy-start | bytes 1156
  279.2 9.6 %collective-permute-start = (bf16[2,15,96]{1,2,0:T(8,128)(2,1)S(1)}, bf16[2,15,96]{1,2,0:T(8,128)(2,1)S(1)}, u32[]{:S(2)}, u32[]{:S(2)}) collective-permute-start(bf16[2,15,96]{1,2,0:T(8,128)(2,1)S(1)} %get-tuple-element.11), channel_id=1, source_target_pairs={{0,16},{16,32},{32,48},{48,64},{64,80},{80,96},{96,112},{112,128},... | collective-permute-start | bytes 17288 | tf_op jit(solution)/shard_map/ppermute | solution.py:19
  282.7 7.7 %collective-permute-start.1 = (bf16[2,15,96]{1,2,0:T(8,128)(2,1)S(1)}, bf16[2,15,96]{1,2,0:T(8,128)(2,1)S(1)}, u32[]{:S(2)}, u32[]{:S(2)}) collective-permute-start(bf16[2,15,96]{1,2,0:T(8,128)(2,1)S(1)} %get-tuple-element.12), channel_id=1, source_target_pairs={{16,0},{32,16},{48,32},{64,48},{80,64},{96,80},{112,96},{128,112},... | collective-permute-start | bytes 17288 | tf_op jit(solution)/shard_map/ppermute | solution.py:21
Sparse Core Ops, SparseCore 0:
  154.4 121.9 all-reduce.1
  294.0 61.8 reduce-scatter.3
where the time goes:
time: 365 us; the launch traced here: 364 us
  waiting for transfers between devices  186 us (51%)
  blocking collectives  88.5 us (24%)
  other arithmetic  32.2 us (9%)
  local copies, waits for them, and re-layouts  19.9 us (5%)
  matrix products  14.8 us (4%)
  between operations  13.6 us (4%)
  starting transfers between devices  9.5 us (3%)
    psum x1, waiting for transfers between devices, shards(): lax.psum(attention_term.astype(jnp.bfloat16), 'tensor').astype(jnp.float32)  122 us
    unnamed x3, waiting for transfers between devices  62 us
    all_gather x1, blocking collectives, shards(): key_piece = lax.all_gather(key_rows, 'tm', axis=1, tiled=True)  46 us
    all_gather x1, blocking collectives, shards(): value_piece = lax.all_gather(value_rows, 'tm', axis=1, tiled=True)  42.4 us
    convert_element_type x1, other arithmetic, positions(): jnp.sin(angles).astype(jnp.bfloat16)  26 us
  transfers between devices with their start and end apart: 4, of which 4 were waited for; matrix products, arithmetic and copies ran while one was open for 0% of the time, Pallas kernels for 0%

commit v1 on v0

--- a/solution.py
+++ b/solution.py
@@ -135,7 +135,9 @@
     )
     row_count = local_rows // lax.axis_size("tensor")
     row_start = lax.axis_index("tensor") * row_count
-    attention_full = lax.psum(attention_term.astype(jnp.bfloat16), "tensor").astype(jnp.float32)
+    attention_full = jnp.sum(
+        lax.all_gather(attention_term.astype(jnp.bfloat16), "tensor"), axis=0
+    ).astype(jnp.float32)
     hidden = (features.astype(jnp.float32) + attention_full).astype(jnp.bfloat16)
     hidden_rows = lax.dynamic_slice_in_dim(hidden, row_start, row_count, 1)
     normed_two = layer_norm(hidden, norm_gains[1]).astype(jnp.bfloat16)

time: 365 us -> 323 us (0.88)
  waiting for transfers between devices: 186 us -> 138 us
  other arithmetic: 32.2 us -> 37.6 us
    psum x1 -> x0, waiting for transfers between devices: 122 us -> none  [shards(): lax.psum(attention_term.astype(jnp.bfloat16), 'tensor').astype(jnp.float32)]
    all_gather x0 -> x1, waiting for transfers between devices: none -> 73.1 us  [shards(): lax.all_gather(attention_term.astype(jnp.bfloat16), 'tensor')]
    reduce_sum x0 -> x1, other arithmetic: none -> 6.66 us  [shards(): jnp.sum(lax.all_gather(attention_term.astype(jnp.bfloat16), 'tensor'), ax...]
where the time goes in v1:
time: 323 us; the launch traced here: 322 us
  waiting for transfers between devices  138 us (43%)
  blocking collectives  88.7 us (27%)
  other arithmetic  37.6 us (12%)
  local copies, waits for them, and re-layouts  20.2 us (6%)
  matrix products  14.8 us (5%)
  between operations  13.7 us (4%)
  starting transfers between devices  9.5 us (3%)
    all_gather x1, waiting for transfers between devices, shards(): lax.all_gather(attention_term.astype(jnp.bfloat16), 'tensor')  73.1 us
    unnamed x3, waiting for transfers between devices  63 us
    all_gather x1, blocking collectives, shards(): key_piece = lax.all_gather(key_rows, 'tm', axis=1, tiled=True)  46 us
    all_gather x1, blocking collectives, shards(): value_piece = lax.all_gather(value_rows, 'tm', axis=1, tiled=True)  42.7 us
    convert_element_type x1, other arithmetic, positions(): jnp.sin(angles).astype(jnp.bfloat16)  26 us
    dot_general x1, matrix products, shards(): jnp.einsum('bqhe,mhe->bhqm', position_q, relative_all, preferred_element_...  6.82 us
    reduce_sum x1, other arithmetic, shards(): jnp.sum(lax.all_gather(attention_term.astype(jnp.bfloat16), 'tensor'), ax...  6.66 us
  transfers between devices with their start and end apart: 4, of which 4 were waited for; matrix products, arithmetic and copies ran while one was open for 0% of the time, Pallas kernels for 0%

profile of v1, /device:TPU:4, one launch (start us, length us, event | category | flops | bytes accessed | tf_op | source)
XLA Modules:
  0.0 322.4 jit_solution(2613347406243466659)
XLA Ops:
  6.5 0.8 slice_reduce_fusion
  7.4 1.3 convert_reduce_fusion
  8.7 1.5 fusion.21
  10.2 0.8 slice_bitcast_fusion.32
  11.0 26.0 %fusion = (bf16[2175,768]{1,0:T(8,128)(2,1)}, bf16[2175,768]{1,0:T(8,128)(2,1)}) fusion(f32[768]{0:T(1024)S(1)} %multiply_exponential_fusion, f32[2175]{0:T(1024)S(1)} %subtract_convert_fusion), kind=kLoop, calls=%fused_computation.2 | loop fusion | flops 5011200 | bytes 6693372 | tf_op jit(solution)/shard_map/convert_element_type | solution.py:43
  38.3 6.8 %convolution_bitcast_fusion = f32[2,1,128,2175]{2,3,0,1:T(8,128)} fusion(bf16[96,1536]{1,0:T(8,128)(2,1)S(1)} %copy-done.8, bf16[2175,768]{1,0:T(8,128)(2,1)} %get-tuple-element.45, bf16[2175,768]{1,0:T(8,128)(2,1)} %get-tuple-element.44, f32[2,128,3,96]{1,3,2,0:T(8,128)S(1)} %get-tuple-element.49, f32[96]{0:T(128)S(1)} %get-tuple-element.47), kind=kOutput, calls=%fused_computation.8 | convolution fusion | flops 761960320 | bytes 9302528 | tf_op jit(solution)/shard_map/bqhe,mhe->bhqm/dot_general | solution.py:115
  45.1 2.0 copy.14
  47.2 4.4 %reshape.176 = f32[2,1,278400]{2,0,1:T(2,128)} reshape(f32[2,1,128,2175]{3,2,0,1:T(8,128)S(1)} %copy.14) | data formatting | bytes 4454400 | tf_op jit(solution)/shard_map/reshape | solution.py:53
  51.5 3.9 %slice.330 = f32[2,1,278272]{2,0,1:T(2,128)S(1)} slice(f32[2,1,278400]{2,0,1:T(2,128)} %reshape.176), slice={[0:2], [0:1], [127:278399]} | slice | bytes 4452352 | tf_op jit(solution)/shard_map/slice | solution.py:54
  55.5 4.5 %reshape.177 = f32[2,1,128,2174]{3,2,0,1:T(8,128)} reshape(f32[2,1,278272]{2,0,1:T(2,128)S(1)} %slice.330) | data formatting | bytes 4452352 | tf_op jit(solution)/shard_map/reshape | solution.py:60
  60.0 46.0 %all-gather = bf16[2,2048,1,96]{1,3,2,0:T(8,128)(2,1)S(1)} all-gather(bf16[2,128,1,96]{1,3,2,0:T(8,128)(2,1)S(1)} %get-tuple-element.10), channel_id=2, replica_groups=mesh['tm'=16,'tensor'=16] {'tm'}, dimensions={1}, use_global_device_ids=true | all-gather | bytes 835584 | tf_op jit(solution)/shard_map/all_gather | solution.py:107
  106.1 2.4 fusion.172
  108.4 42.7 %all-gather.1 = bf16[2,2048,1,96]{1,3,2,0:T(8,128)(2,1)} all-gather(bf16[2,128,1,96]{1,3,2,0:T(8,128)(2,1)S(1)} %get-tuple-element.9), channel_id=3, replica_groups=mesh['tm'=16,'tensor'=16] {'tm'}, dimensions={1}, use_global_device_ids=true | all-gather | bytes 835584 | tf_op jit(solution)/shard_map/all_gather | solution.py:108
  151.7 2.9 convolution_convert_fusion.1
  154.8 73.1 %all-gather.5.cloned.1.call-done = bf16[32,128,1536]{2,1,0:T(8,128)(2,1)} async-done(((bf16[2,128,1536]{2,1,0:T(8,128)(2,1)}), bf16[32,128,1536]{2,1,0:T(8,128)(2,1)}) %all-gather.5.cloned.1.call-update) | async-done | bytes 12582928 | tf_op jit(solution)/shard_map/all_gather | solution.py:139
  227.9 6.7 %reduce_sum.60 = bf16[2,128,1536]{2,1,0:T(8,128)(2,1)S(1)} reduce(bf16[16,2,128,1536]{3,2,1,0:T(8,128)(2,1)} %bitcast.147, bf16[]{:T(256)} %constant.36.clone.1), dimensions={0}, to_apply=%region_4.5 | reduce | flops 5898240 | bytes 13369346 | tf_op jit(solution)/shard_map/reduce_sum | solution.py:138
  236.3 3.5 %collective-permute-start = (bf16[2,15,96]{1,2,0:T(8,128)(2,1)S(1)}, bf16[2,15,96]{1,2,0:T(8,128)(2,1)S(1)}, u32[]{:S(2)}, u32[]{:S(2)}) collective-permute-start(bf16[2,15,96]{1,2,0:T(8,128)(2,1)S(1)} %get-tuple-element.11), channel_id=1, source_target_pairs={{0,16},{16,32},{32,48},{48,64},{64,80},{80,96},{96,112},{112,128},... | collective-permute-start | bytes 17288 | tf_op jit(solution)/shard_map/ppermute | solution.py:19
  239.8 6.0 %collective-permute-start.1 = (bf16[2,15,96]{1,2,0:T(8,128)(2,1)S(1)}, bf16[2,15,96]{1,2,0:T(8,128)(2,1)S(1)}, u32[]{:S(2)}, u32[]{:S(2)}) collective-permute-start(bf16[2,15,96]{1,2,0:T(8,128)(2,1)S(1)} %get-tuple-element.12), channel_id=1, source_target_pairs={{16,0},{32,16},{48,32},{64,48},{80,64},{96,80},{112,96},{128,112},... | collective-permute-start | bytes 17288 | tf_op jit(solution)/shard_map/ppermute | solution.py:21
  245.9 1.6 collective-permute-done.1
  247.5 1.7 convolution_convert_fusion
  249.2 0.8 copy.17
  250.0 1.0 copy.19
  251.1 63.0 %reduce-scatter.4.cloned.1.call-done = bf16[8,3072]{1,0:T(8,128)(2,1)} async-done(((bf16[128,3072]{1,0:T(8,128)(2,1)}), bf16[8,3072]{1,0:T(8,128)(2,1)}) %reduce-scatter.4.cloned.1.call-update) | async-done | bytes 49168
  314.0 0.8 reshape.191
  (50 shorter events, 4.5 us)
Async XLA Ops:
  6.5 30.5 %copy-start = (bf16[3,96,1536]{2,1,0:T(8,128)(2,1)S(1)}, bf16[3,96,1536]{2,1,0:T(8,128)(2,1)}, u32[]{:S(2)}) copy-start(bf16[3,96,1536]{2,1,0:T(8,128)(2,1)} %param.15) | copy-start | bytes 2654212
  6.5 221.4 %all-gather.5.cloned.1.call-start = ((), (), s32[]{:S(2)}) async-start(), calls=%async_computation.1 | async-start | bytes 13369344 | tf_op jit(solution)/shard_map/all_gather | solution.py:139
  11.0 26.0 %copy-start.1 = (bf16[2,128,1536]{2,1,0:T(8,128)(2,1)S(1)}, bf16[2,128,1536]{2,1,0:T(8,128)(2,1)}, u32[]{:S(2)}) copy-start(bf16[2,128,1536]{2,1,0:T(8,128)(2,1)} %param.12) | copy-start | bytes 2359300
  37.0 1.3 copy-start.8
  37.6 0.7 copy-start.4
  55.5 50.5 %copy-start.6 = (s32[2]{0:T(128)S(1)}, s32[2]{0:T(128)}, u32[]{:S(2)}) copy-start(s32[2]{0:T(128)} %param.13) | copy-start | bytes 28
  108.4 43.2 %copy-start.3 = (bf16[96,1536]{1,0:T(8,128)(2,1)S(1)}, bf16[96,1536]{1,0:T(8,128)(2,1)}, u32[]{:S(2)}) copy-start(bf16[96,1536]{1,0:T(8,128)(2,1)} %param.18) | copy-start | bytes 884740
  151.7 3.1 copy-start.5
  154.6 159.4 %reduce-scatter.4.cloned.1.call-start = ((), (), s32[]{:S(2)}) async-start(), calls=%async_computation.2 | async-start | bytes 835584
  227.9 6.7 %copy-start.2 = (bf16[2,128,1536]{2,1,0:T(8,128)(2,1)S(1)}, bf16[2,128,1536]{2,1,0:T(8,128)(2,1)}, u32[]{:S(2)}) copy-start(bf16[2,128,1536]{2,1,0:T(8,128)(2,1)} %param.12) | copy-start | bytes 2359300
  234.6 1.1 copy-start.7
  234.9 12.6 %copy-start.9 = (bf16[96,1536]{1,0:T(8,128)(2,1)S(1)}, bf16[96,1536]{1,0:T(8,128)(2,1)}, u32[]{:S(2)}) copy-start(bf16[96,1536]{1,0:T(8,128)(2,1)} %param.23) | copy-start | bytes 884740
  234.9 12.6 %copy-start.10 = (f32[96]{0:T(128)S(1)}, f32[96]{0:T(128)}, u32[]{:S(2)}) copy-start(f32[96]{0:T(128)} %param.22) | copy-start | bytes 1156
  234.9 12.6 %copy-start.11 = (f32[96]{0:T(128)S(1)}, f32[96]{0:T(128)}, u32[]{:S(2)}) copy-start(f32[96]{0:T(128)} %param.21) | copy-start | bytes 1156
  236.3 9.6 %collective-permute-start = (bf16[2,15,96]{1,2,0:T(8,128)(2,1)S(1)}, bf16[2,15,96]{1,2,0:T(8,128)(2,1)S(1)}, u32[]{:S(2)}, u32[]{:S(2)}) collective-permute-start(bf16[2,15,96]{1,2,0:T(8,128)(2,1)S(1)} %get-tuple-element.11), channel_id=1, source_target_pairs={{0,16},{16,32},{32,48},{48,64},{64,80},{80,96},{96,112},{112,128},... | collective-permute-start | bytes 17288 | tf_op jit(solution)/shard_map/ppermute | solution.py:19
  239.8 7.7 %collective-permute-start.1 = (bf16[2,15,96]{1,2,0:T(8,128)(2,1)S(1)}, bf16[2,15,96]{1,2,0:T(8,128)(2,1)S(1)}, u32[]{:S(2)}, u32[]{:S(2)}) collective-permute-start(bf16[2,15,96]{1,2,0:T(8,128)(2,1)S(1)} %get-tuple-element.12), channel_id=1, source_target_pairs={{16,0},{32,16},{48,32},{64,48},{80,64},{96,80},{112,96},{128,112},... | collective-permute-start | bytes 17288 | tf_op jit(solution)/shard_map/ppermute | solution.py:21
Sparse Core Ops, SparseCore 0:
  154.8 73.0 all-gather.4
  251.2 62.8 reduce-scatter.3
